TPU v7x, 32 devices: a whole 2x2x4 slice. The times are simulated.
32 devices in a mesh: section: 4 (over x, core), dom: 8 (over z, y).
Axes of the slice: x: 2, y: 2, z: 4, core: 2. Of those that a mesh axis runs over, the one named last changes fastest.
Arguments:
- node_latents: bfloat16 [4, 8192, 512], P('section', 'dom'), may hold values from -6 to 6
- edge_latents: bfloat16 [4, 12288, 512], P('section', 'dom'), may hold values from -6 to 6
- entering_nodes: bfloat16 [8192, 512], P('dom'), may hold values from -6 to 6
- entering_edges: bfloat16 [12288, 512], P('dom'), may hold values from -6 to 6
- edge_first: bfloat16 [4, 1536, 512], P('section'), may hold values from -0.15625 to 0.15625
- edge_second: bfloat16 [4, 512, 512], P('section'), may hold values from -0.25 to 0.25
- edge_gain: float32 [4, 512], P('section'), may hold values from 0.1 to 1.9
- node_first: bfloat16 [4, 1024, 512], P('section'), may hold values from -0.1875 to 0.1875
- node_second: bfloat16 [4, 512, 512], P('section'), may hold values from -0.25 to 0.25
- node_gain: float32 [4, 512], P('section'), may hold values from 0.1 to 1.9
- pair_list: int32 [8, 12, 3], P('dom'), may hold values from 0 to 7, as said below
- send_list: int32 [8, 4], P('dom'), may hold values from 0 to 7, as said below
- senders: int32 [12288, 128], P('dom'), may hold values from 0 to 1, as said below
- receivers: int32 [12288, 128], P('dom'), may hold values from 0 to 1, as said below
Outputs:
- final_nodes: bfloat16 [4, 8192, 512], P('section', 'dom')
- final_edges: bfloat16 [4, 12288, 512], P('section', 'dom')
Inputs may be any that keep to these rules, and one draw needn't show every extreme that they name: `pair_list`: columns 0 and 2 are node block numbers below 8, column 1 a partner code 0 to 4 (0: sender block on the same partition); every partition lists each code 1 to 4 at least once and names each of its node blocks in column 0 at least once. `send_list`: node block numbers below 8. `senders`: each row has exactly one 1. `receivers`: each row has exactly one 1.
All inputs are finite; a program needn't handle non-finite values.
Results may differ from a plain program's by a relative error of at most 0.0075.
Values may be sent and summed in bfloat16 or wider, within the bound.
No kernel may reach another device: no remote copies, remote signals or barrier semaphores. Data moves between devices by JAX's collectives and lax.ppermute only.
A program may use at most 128 MiB of HBM per device.

v0:
```python
import functools

import jax
import jax.numpy as jnp
from jax import lax
from jax.experimental import pallas as pl
from jax.experimental.pallas import tpu as pltpu
from jax.sharding import PartitionSpec as P

partner_offsets = (1, -1, 2, -2)
epsilon = 1e-05
f32 = jnp.float32
bf16 = jnp.bfloat16
VMEM = pl.BlockSpec(memory_space=pltpu.VMEM)
SMEM = pl.BlockSpec(memory_space=pltpu.SMEM)


def passed_along(block, axis, distance):
    devices = range(lax.axis_size(axis))
    route = [((i - distance) % len(devices), i) for i in devices]
    return lax.ppermute(block, axis, route)


def from_behind(value, axis):
    count = lax.axis_size(axis)
    return lax.ppermute(value, axis, [(source, source + 1) for source in range(count - 1)])


def layer_norm(values, gain):
    centred = values - jnp.mean(values, axis=-1, keepdims=True)
    spread = jnp.mean(centred * centred, axis=-1, keepdims=True)
    return centred * lax.rsqrt(spread + epsilon) * gain


def product(left, right):
    return jnp.dot(left, right, preferred_element_type=f32)


def call(kernel, name, outs, ins, operands, scratch=(), flops=0, moved=0):
    return pl.pallas_call(
        kernel,
        name=name,
        out_shape=outs,
        in_specs=ins,
        out_specs=jax.tree.map(lambda _: VMEM, outs),
        scratch_shapes=list(scratch),
        compiler_params=pltpu.CompilerParams(vmem_limit_bytes=60 << 20),
        cost_estimate=pl.CostEstimate(flops=flops, bytes_accessed=moved, transcendentals=0),
    )(*operands)


def shape(dims, kind):
    return jax.ShapeDtypeStruct(dims, kind)


def pick_kernel(sends, nodes, *outs):
    rows = outs[0].shape[0]
    for slot in range(4):
        start = pl.multiple_of(sends[slot] * rows, rows)
        outs[slot][...] = nodes[pl.ds(start, rows), :]


def pick_select_kernel(flag, sends, entering, moved, nodes, *outs):
    rows = outs[0].shape[0]

    @pl.when(flag[0] == 0)
    def _():
        nodes[...] = entering[...]

    @pl.when(flag[0] != 0)
    def _():
        nodes[...] = moved[...]

    for slot in range(4):
        start = pl.multiple_of(sends[slot] * rows, rows)
        outs[slot][...] = nodes[pl.ds(start, rows), :]


def ends_kernel(senders, receivers, ends, flipped):
    rows = senders.shape[1]
    for block in range(senders.shape[0] // rows):
        here = pl.ds(block * rows, rows)
        for side, source in enumerate((senders, receivers)):
            part = source[here, :].astype(f32)
            ends[here, side * rows : (side + 1) * rows] = part.astype(bf16)
            flipped[pl.ds((2 * block + side) * rows, rows), :] = part.T.astype(bf16)


def project_kernel(edges, nodes, edge_first, base, sent, received):
    width = nodes.shape[1]
    base[...] = product(edges[...], edge_first[:width, :])
    sent[...] = product(nodes[...], edge_first[width : 2 * width, :]).astype(bf16)
    received[...] = product(nodes[...], edge_first[2 * width :, :]).astype(bf16)


def project_select_kernel(flag, entering, moved, nodes, edge_first, edges, base, sent, received):
    @pl.when(flag[0] == 0)
    def _():
        edges[...] = entering[...]

    @pl.when(flag[0] != 0)
    def _():
        edges[...] = moved[...]

    project_kernel(edges, nodes, edge_first, base, sent, received)


def edge_kernel(
    pairs,
    in_one,
    in_two,
    in_three,
    in_four,
    base,
    sent,
    received,
    ends,
    flipped,
    edges,
    edge_first,
    edge_second,
    gain,
    new_edges,
    own,
    out_one,
    out_two,
    out_three,
    out_four,
    lookup,
    sums,
):
    rows, width = in_one.shape
    blocks = sent.shape[0] // rows
    number = edges.shape[0] // rows
    lookup[: blocks * rows, :] = sent[...]
    middle = edge_first[width : 2 * width, :]
    for slot, block in enumerate((in_one, in_two, in_three, in_four)):
        lookup[(blocks + slot) * rows : (blocks + slot + 1) * rows, :] = product(
            block[...], middle
        ).astype(bf16)
    sums[...] = jnp.zeros_like(sums)
    group = 4 if number % 4 == 0 else 1
    for first in range(0, number, group):
        hidden = []
        places = []
        for block in range(first, first + group):
            code = pairs[block, 1]
            source = jnp.where(code == 0, pairs[block, 2], blocks + code - 1)
            source = pl.multiple_of(source * rows, rows)
            target = pl.multiple_of(pairs[block, 0] * rows, rows)
            places.append((source, target))
            both = jnp.concatenate(
                [lookup[pl.ds(source, rows), :], received[pl.ds(target, rows), :]], axis=0
            )
            here = slice(block * rows, (block + 1) * rows)
            summed = base[here, :] + product(ends[here, :], both)
            hidden.append(jnp.maximum(summed, 0.0).astype(bf16))
        message = layer_norm(product(jnp.concatenate(hidden, axis=0), edge_second[...]), gain[...])
        span = slice(first * rows, (first + group) * rows)
        new_edges[span, :] = (edges[span, :].astype(f32) + message).astype(bf16)
        low = message.astype(bf16)
        for index, (source, target) in enumerate(places):
            block = first + index
            spread = product(
                flipped[2 * block * rows : 2 * (block + 1) * rows, :],
                low[index * rows : (index + 1) * rows, :],
            )
            sums[pl.ds(source, rows), :] += spread[:rows, :]
            sums[pl.ds(target, rows), :] += spread[rows:, :]
    own[...] = sums[: blocks * rows, :]
    for slot, out in enumerate((out_one, out_two, out_three, out_four)):
        out[...] = sums[(blocks + slot) * rows : (blocks + slot + 1) * rows, :].astype(bf16)


def ready_kernel(nodes, node_first, partial):
    partial[...] = product(nodes[...], node_first[: nodes.shape[1], :])


def node_kernel(
    sends,
    back_one,
    back_two,
    back_three,
    back_four,
    own,
    partial,
    nodes,
    node_first,
    node_second,
    gain,
    new_nodes,
    total,
):
    rows, width = back_one.shape
    total[...] = own[...]
    for slot, block in enumerate((back_one, back_two, back_three, back_four)):
        start = pl.multiple_of(sends[slot] * rows, rows)
        total[pl.ds(start, rows), :] += block[...].astype(f32)
    hidden = partial[...] + product(total[...].astype(bf16), node_first[width:, :])
    hidden = jnp.maximum(hidden, 0.0).astype(bf16)
    update = layer_norm(product(hidden, node_second[...]), gain[...])
    new_nodes[...] = (nodes[...].astype(f32) + update).astype(bf16)


def local(
    node_latents,
    edge_latents,
    entering_nodes,
    entering_edges,
    edge_first,
    edge_second,
    edge_gain,
    node_first,
    node_second,
    node_gain,
    pair_list,
    send_list,
    senders,
    receivers,
):
    edge_first, edge_second, node_first, node_second = (
        edge_first[0],
        edge_second[0],
        node_first[0],
        node_second[0],
    )
    pairs = pair_list[0]
    sends = send_list[0]
    flag = lax.axis_index("section").astype(jnp.int32).reshape(1)
    node_rows, width = entering_nodes.shape
    edge_rows = entering_edges.shape[0]
    rows = senders.shape[1]
    block = shape((rows, width), bf16)
    ends, flipped = None, None

    def tick(nodes, edges, picked, ends, flipped, projected):
        incoming = [passed_along(picked[i], "dom", partner_offsets[i]) for i in range(4)]
        if ends is None:
            ends, flipped = call(
                ends_kernel,
                "ends",
                (shape((edge_rows, 2 * rows), bf16), shape((2 * edge_rows, rows), bf16)),
                [VMEM] * 2,
                (senders, receivers),
                flops=10**8,
                moved=3 << 20,
            )
        edges, base, sent, received = projected(nodes)
        new_edges, own, *partials = call(
            edge_kernel,
            "edge",
            (
                shape((edge_rows, width), bf16),
                shape((node_rows, width), f32),
                block,
                block,
                block,
                block,
            ),
            [SMEM] + [VMEM] * 13,
            (
                pairs,
                *incoming,
                base,
                sent,
                received,
                ends,
                flipped,
                edges,
                edge_first,
                edge_second,
                edge_gain,
            ),
            scratch=(
                pltpu.VMEM((node_rows + 4 * rows, width), bf16),
                pltpu.VMEM((node_rows + 4 * rows, width), f32),
            ),
            flops=4 * 10**9,
            moved=12 << 20,
        )
        returned = [passed_along(partials[i], "dom", -partner_offsets[i]) for i in range(4)]
        partial = call(
            ready_kernel,
            "ready",
            shape((node_rows, width), f32),
            [VMEM] * 2,
            (nodes, node_first),
            flops=2 * node_rows * width * width,
            moved=3 << 20,
        )
        new_nodes = call(
            node_kernel,
            "node",
            shape((node_rows, width), bf16),
            [SMEM] + [VMEM] * 10,
            (
                sends,
                *returned,
                own,
                partial,
                nodes,
                node_first,
                node_second,
                node_gain,
            ),
            scratch=(pltpu.VMEM((node_rows, width), f32),),
            flops=4 * node_rows * width * width,
            moved=8 << 20,
        )
        return new_nodes, new_edges, ends, flipped

    project_outs = (
        shape((edge_rows, width), f32),
        shape((node_rows, width), bf16),
        shape((node_rows, width), bf16),
    )
    project_cost = dict(flops=2 * (edge_rows + 2 * node_rows) * width * width, moved=9 << 20)
    nodes, edges = node_latents[0], edge_latents[0]
    picked = call(pick_kernel, "pick", (block,) * 4, [SMEM, VMEM], (sends, nodes))

    def project_now(nodes):
        return edges, *call(
            project_kernel,
            "project",
            project_outs,
            [VMEM] * 3,
            (edges, nodes, edge_first),
            **project_cost,
        )

    nodes, new_edges, ends, flipped = tick(nodes, edges, picked, None, None, project_now)
    moved_nodes = from_behind(nodes, "section")
    moved_edges = from_behind(new_edges, "section")
    nodes, *picked = call(
        pick_select_kernel,
        "pick_select",
        (shape((node_rows, width), bf16),) + (block,) * 4,
        [SMEM] * 2 + [VMEM] * 2,
        (flag, sends, entering_nodes, moved_nodes),
    )

    def project_later(nodes):
        return call(
            project_select_kernel,
            "project_select",
            (shape((edge_rows, width), bf16),) + project_outs,
            [SMEM] + [VMEM] * 4,
            (flag, entering_edges, moved_edges, nodes, edge_first),
            **project_cost,
        )

    nodes, new_edges, _, _ = tick(nodes, None, picked, ends, flipped, project_later)
    return (nodes[None], new_edges[None])


def solution(mesh):
    placed = (
        P("section", "dom", None),
        P("section", "dom", None),
        P("dom", None),
        P("dom", None),
        P("section", None, None),
        P("section", None, None),
        P("section", None),
        P("section", None, None),
        P("section", None, None),
        P("section", None),
        P("dom", None, None),
        P("dom", None),
        P("dom", None),
        P("dom", None),
    )
    return jax.shard_map(
        local,
        mesh=mesh,
        in_specs=placed,
        out_specs=(P("section", "dom", None), P("section", "dom", None)),
        check_vma=False,
    )
```

profile of v0, /device:TPU:6, one launch (start us, length us, event | category | flops | bytes accessed | tf_op | source)
XLA Modules:
  0.0 118.2 jit_solution(16053656035607310428)
XLA Ops:
  0.6 2.0 %pick.1 = (bf16[128,512]{1,0:T(8,128)(2,1)}, bf16[128,512]{1,0:T(8,128)(2,1)}, bf16[128,512]{1,0:T(8,128)(2,1)}, bf16[128,512]{1,0:T(8,128)(2,1)}) custom-call(s32[4]{0:T(128)} %bitcast.24, bf16[1024,512]{1,0:T(8,128)(2,1)} %bitcast.15), custom_call_target="tpu_custom_call" | custom-call | tf_op jit(solution)/shard_map/pick/pallas_call | solution.py:40
  2.7 1.5 %collective-permute-start = (bf16[128,512]{1,0:T(8,128)(2,1)}, bf16[128,512]{1,0:T(8,128)(2,1)S(1)}, u32[]{:S(2)}, u32[]{:S(2)}) collective-permute-start(bf16[128,512]{1,0:T(8,128)(2,1)} %get-tuple-element.32), channel_id=1, source_target_pairs={{7,0},{0,1},{1,2},{2,3},{3,4},{4,5},{5,6},{6,7},{15,8},{8,9},{9,10... | collective-permute-start | bytes 393224 | tf_op jit(solution)/shard_map/ppermute | solution.py:21
  4.2 0.5 collective-permute-start.1
  4.7 1.6 %collective-permute-start.2 = (bf16[128,512]{1,0:T(8,128)(2,1)}, bf16[128,512]{1,0:T(8,128)(2,1)S(1)}, u32[]{:S(2)}, u32[]{:S(2)}) collective-permute-start(bf16[128,512]{1,0:T(8,128)(2,1)} %get-tuple-element.34), channel_id=1, source_target_pairs={{6,0},{7,1},{0,2},{1,3},{2,4},{3,5},{4,6},{5,7},{14,8},{15,9},{8,1... | collective-permute-start | bytes 393224 | tf_op jit(solution)/shard_map/ppermute | solution.py:21
  6.3 2.2 %collective-permute-start.3 = (bf16[128,512]{1,0:T(8,128)(2,1)}, bf16[128,512]{1,0:T(8,128)(2,1)S(1)}, u32[]{:S(2)}, u32[]{:S(2)}) collective-permute-start(bf16[128,512]{1,0:T(8,128)(2,1)} %get-tuple-element.35), channel_id=1, source_target_pairs={{2,0},{3,1},{4,2},{5,3},{6,4},{7,5},{0,6},{1,7},{10,8},{11,9},{12,... | collective-permute-start | bytes 393224 | tf_op jit(solution)/shard_map/ppermute | solution.py:21
  8.5 1.4 %copy.18 = s32[1,12,3]{2,1,0:T(8,128)} copy(s32[1,12,3]{1,0,2:T(1,128)} %param.24) | data formatting | bytes 288 | tf_op jit(solution)/shard_map/squeeze | solution.py:227
  9.9 2.7 %ends.1 = (bf16[1536,256]{1,0:T(8,128)(2,1)}, bf16[3072,128]{1,0:T(8,128)(2,1)}) custom-call(s32[1536,128]{1,0:T(8,128)} %senders.1, s32[1536,128]{1,0:T(8,128)} %receivers.1), custom_call_target="tpu_custom_call" | custom-call | flops 100000000 | bytes 3145728 | tf_op jit(solution)/shard_map/ends/pallas_call | solution.py:40
  12.6 5.6 %project.1 = (f32[1536,512]{1,0:T(8,128)}, bf16[1024,512]{1,0:T(8,128)(2,1)}, bf16[1024,512]{1,0:T(8,128)(2,1)}) custom-call(bf16[1536,512]{1,0:T(8,128)(2,1)} %bitcast.28, bf16[1024,512]{1,0:T(8,128)(2,1)} %bitcast.16, bf16[1536,512]{1,0:T(8,128)(2,1)} %bitcast.30), custom_call_target="tpu_custom_call" | custom-call | flops 1879048192 | bytes 9437184 | tf_op jit(solution)/shard_map/project/pallas_call | solution.py:40
  18.2 0.0 collective-permute-done.in_one
  18.2 0.0 collective-permute-done.1.in_two
  18.2 0.0 copy-start.14
  18.2 0.0 collective-permute-done.2.in_three
  18.2 0.0 collective-permute-done.3.in_four
  18.2 0.6 copy-done.12
  18.8 0.0 copy-done.14
  18.9 0.1 copy-done.16
  18.9 0.1 copy-done.17
  19.0 10.3 %edge.2 = (bf16[1536,512]{1,0:T(8,128)(2,1)}, f32[1024,512]{1,0:T(8,128)}, bf16[128,512]{1,0:T(8,128)(2,1)}, bf16[128,512]{1,0:T(8,128)(2,1)}, bf16[128,512]{1,0:T(8,128)(2,1)}, /*index=5*/bf16[128,512]{1,0:T(8,128)(2,1)}) custom-call(s32[12,3]{1,0:T(8,128)} %bitcast.22, bf16[128,512]{1,0:T(8,128)(2,1)} %copy-done.12, bf16[128,512]{1,0:T(8,128)(2,1)} %copy-done.14, ...), custom_call_target="tpu_custom_call" | custom-call | flops 4000000000 | bytes 12582912 | tf_op jit(solution)/shard_map/edge/pallas_call | solution.py:40
  29.3 1.9 %collective-permute-start.13 = (bf16[1536,512]{1,0:T(8,128)(2,1)}, bf16[1536,512]{1,0:T(8,128)(2,1)S(1)}, u32[]{:S(2)}, u32[]{:S(2)}) collective-permute-start(bf16[1536,512]{1,0:T(8,128)(2,1)} %get-tuple-element.50), channel_id=1, source_target_pairs={{0,8},{8,16},{16,24},{1,9},{9,17},{17,25},{2,10},{10,18},{18,26},{... | collective-permute-start | bytes 4718600 | tf_op jit(solution)/shard_map/ppermute | solution.py:26
  31.3 3.3 %collective-permute-start.4 = (bf16[128,512]{1,0:T(8,128)(2,1)}, bf16[128,512]{1,0:T(8,128)(2,1)S(1)}, u32[]{:S(2)}, u32[]{:S(2)}) collective-permute-start(bf16[128,512]{1,0:T(8,128)(2,1)} %get-tuple-element.41), channel_id=1, source_target_pairs={{1,0},{2,1},{3,2},{4,3},{5,4},{6,5},{7,6},{0,7},{9,8},{10,9},{11,1... | collective-permute-start | bytes 393224 | tf_op jit(solution)/shard_map/ppermute | solution.py:21
  34.5 0.0 collective-permute-start.5
  34.5 3.3 %collective-permute-start.6 = (bf16[128,512]{1,0:T(8,128)(2,1)}, bf16[128,512]{1,0:T(8,128)(2,1)S(1)}, u32[]{:S(2)}, u32[]{:S(2)}) collective-permute-start(bf16[128,512]{1,0:T(8,128)(2,1)} %get-tuple-element.43), channel_id=1, source_target_pairs={{2,0},{3,1},{4,2},{5,3},{6,4},{7,5},{0,6},{1,7},{10,8},{11,9},{12,... | collective-permute-start | bytes 393224 | tf_op jit(solution)/shard_map/ppermute | solution.py:21
  37.8 0.0 collective-permute-start.7
  37.9 3.6 %ready.2.partial = f32[1024,512]{1,0:T(8,128)} custom-call(bf16[1024,512]{1,0:T(8,128)(2,1)} %bitcast.17, bf16[1024,512]{1,0:T(8,128)(2,1)} %bitcast.11), custom_call_target="tpu_custom_call" | custom-call | flops 536870912 | bytes 3145728 | tf_op jit(solution)/shard_map/ready/pallas_call | solution.py:40
  41.5 0.0 collective-permute-done.4.back_one
  41.5 0.0 collective-permute-done.5.back_two
  41.5 0.1 collective-permute-done.6.back_three
  41.5 3.7 %collective-permute-done.7.back_four = bf16[128,512]{1,0:T(8,128)(2,1)S(1)} collective-permute-done((bf16[128,512]{1,0:T(8,128)(2,1)}, bf16[128,512]{1,0:T(8,128)(2,1)S(1)}, u32[]{:S(2)}, u32[]{:S(2)}) %collective-permute-start.7) | collective-permute-done | bytes 131104 | tf_op jit(solution)/shard_map/ppermute | solution.py:21
  45.3 0.0 copy-done.3
  45.3 0.6 copy-done.7
  45.9 6.0 %node.2 = bf16[1024,512]{1,0:T(8,128)(2,1)} custom-call(s32[4]{0:T(128)} %bitcast.25, bf16[128,512]{1,0:T(8,128)(2,1)} %copy-done.1, bf16[128,512]{1,0:T(8,128)(2,1)} %copy-done.3, bf16[128,512]{1,0:T(8,128)(2,1)} %copy-done.5, bf16[128,512]{1,0:T(8,128)(2,1)} %copy-done.7, f32[1024,512]{1,0:T(8,128)} %get-tuple-element.45.own, f32[1024,512]{1,0:T(8,128)} %ready.2.partial, ...), custom_call_target="tpu_custom_call" | custom-call | flops 1073741824 | bytes 8388608 | tf_op jit(solution)/shard_map/node/pallas_call | solution.py:40
  52.0 1.9 %collective-permute-start.8 = (bf16[1024,512]{1,0:T(8,128)(2,1)}, bf16[1024,512]{1,0:T(8,128)(2,1)S(1)}, u32[]{:S(2)}, u32[]{:S(2)}) collective-permute-start(bf16[1024,512]{1,0:T(8,128)(2,1)} %node.2), channel_id=1, source_target_pairs={{0,8},{8,16},{16,24},{1,9},{9,17},{17,25},{2,10},{10,18},{18,26},{... | collective-permute-start | bytes 3145736 | tf_op jit(solution)/shard_map/ppermute | solution.py:26
  53.9 14.9 %collective-permute-done.8.moved = bf16[1024,512]{1,0:T(8,128)(2,1)S(1)} collective-permute-done((bf16[1024,512]{1,0:T(8,128)(2,1)}, bf16[1024,512]{1,0:T(8,128)(2,1)S(1)}, u32[]{:S(2)}, u32[]{:S(2)}) %collective-permute-start.8) | collective-permute-done | bytes 1048608 | tf_op jit(solution)/shard_map/ppermute | solution.py:26
  68.8 1.0 copy-done
  69.7 2.9 %pick_select.1 = (bf16[1024,512]{1,0:T(8,128)(2,1)}, bf16[128,512]{1,0:T(8,128)(2,1)}, bf16[128,512]{1,0:T(8,128)(2,1)}, bf16[128,512]{1,0:T(8,128)(2,1)}, bf16[128,512]{1,0:T(8,128)(2,1)}) custom-call(s32[1]{0:T(128)} %bitcast.2.flag, s32[4]{0:T(128)} %bitcast.26, bf16[1024,512]{1,0:T(8,128)(2,1)} %entering.2, bf16[1024,512]{1,0:T(8,128)(2,1)} %copy-done), custom_call_target="tpu_custom_call" | custom-call | tf_op jit(solution)/shard_map/pick_select/pallas_call | solution.py:40
  72.6 0.0 collective-permute-start.10
  72.6 0.0 collective-permute-start.11
  72.6 3.8 %collective-permute-start.12 = (bf16[128,512]{1,0:T(8,128)(2,1)}, bf16[128,512]{1,0:T(8,128)(2,1)S(1)}, u32[]{:S(2)}, u32[]{:S(2)}) collective-permute-start(bf16[128,512]{1,0:T(8,128)(2,1)} %get-tuple-element.49), channel_id=1, source_target_pairs={{2,0},{3,1},{4,2},{5,3},{6,4},{7,5},{0,6},{1,7},{10,8},{11,9},{12,... | collective-permute-start | bytes 393224 | tf_op jit(solution)/shard_map/ppermute | solution.py:21
  76.4 1.1 collective-permute-start.9
  77.6 0.0 collective-permute-done.13.moved
  77.6 1.1 copy-done.9
  78.7 6.3 %project_select.1 = (bf16[1536,512]{1,0:T(8,128)(2,1)}, f32[1536,512]{1,0:T(8,128)}, bf16[1024,512]{1,0:T(8,128)(2,1)}, bf16[1024,512]{1,0:T(8,128)(2,1)}) custom-call(s32[1]{0:T(128)} %bitcast.2.flag, bf16[1536,512]{1,0:T(8,128)(2,1)} %entering.3, bf16[1536,512]{1,0:T(8,128)(2,1)} %copy-done.9, bf16[1024,512]{1,0:T(8,128)(2,1)} %get-tuple-element.51.nodes, ...), custom_call_target="tpu_custom_call" | custom-call | flops 1879048192 | bytes 9437184 | tf_op jit(solution)/shard_map/project_select/pallas_call | solution.py:40
  85.1 0.0 collective-permute-done.10.in_two
  85.1 0.0 collective-permute-done.11.in_three
  85.1 0.0 copy-start.11
  85.1 0.0 collective-permute-done.12.in_four
  85.1 0.0 collective-permute-done.9.in_one
  85.1 0.6 copy-done.10
  85.7 0.0 copy-done.11
  85.8 0.1 copy-done.13
  85.8 0.1 copy-done.15
  85.9 10.3 %edge.3 = (bf16[1536,512]{1,0:T(8,128)(2,1)}, f32[1024,512]{1,0:T(8,128)}, bf16[128,512]{1,0:T(8,128)(2,1)}, bf16[128,512]{1,0:T(8,128)(2,1)}, bf16[128,512]{1,0:T(8,128)(2,1)}, /*index=5*/bf16[128,512]{1,0:T(8,128)(2,1)}) custom-call(s32[12,3]{1,0:T(8,128)} %bitcast.23, bf16[128,512]{1,0:T(8,128)(2,1)} %copy-done.15, bf16[128,512]{1,0:T(8,128)(2,1)} %copy-done.10, ...), custom_call_target="tpu_custom_call" | custom-call | flops 4000000000 | bytes 12582912 | tf_op jit(solution)/shard_map/edge/pallas_call | solution.py:40
  96.2 0.9 collective-permute-start.14
  97.1 2.0 %collective-permute-start.15 = (bf16[128,512]{1,0:T(8,128)(2,1)}, bf16[128,512]{1,0:T(8,128)(2,1)S(1)}, u32[]{:S(2)}, u32[]{:S(2)}) collective-permute-start(bf16[128,512]{1,0:T(8,128)(2,1)} %get-tuple-element.57), channel_id=1, source_target_pairs={{7,0},{0,1},{1,2},{2,3},{3,4},{4,5},{5,6},{6,7},{15,8},{8,9},{9,10... | collective-permute-start | bytes 393224 | tf_op jit(solution)/shard_map/ppermute | solution.py:21
  99.1 5.4 %collective-permute-start.16 = (bf16[128,512]{1,0:T(8,128)(2,1)}, bf16[128,512]{1,0:T(8,128)(2,1)S(1)}, u32[]{:S(2)}, u32[]{:S(2)}) collective-permute-start(bf16[128,512]{1,0:T(8,128)(2,1)} %get-tuple-element.58), channel_id=1, source_target_pairs={{2,0},{3,1},{4,2},{5,3},{6,4},{7,5},{0,6},{1,7},{10,8},{11,9},{12,... | collective-permute-start | bytes 393224 | tf_op jit(solution)/shard_map/ppermute | solution.py:21
  104.6 0.0 collective-permute-start.17
  104.6 3.6 %ready.3.partial = f32[1024,512]{1,0:T(8,128)} custom-call(bf16[1024,512]{1,0:T(8,128)(2,1)} %get-tuple-element.51.nodes, bf16[1024,512]{1,0:T(8,128)(2,1)} %bitcast.13), custom_call_target="tpu_custom_call" | custom-call | flops 536870912 | bytes 3145728 | tf_op jit(solution)/shard_map/ready/pallas_call | solution.py:40
  108.2 0.0 collective-permute-done.14.back_one
  108.2 0.0 collective-permute-done.15.back_two
  108.2 0.0 collective-permute-done.16.back_three
  108.2 3.3 %collective-permute-done.17.back_four = bf16[128,512]{1,0:T(8,128)(2,1)S(1)} collective-permute-done((bf16[128,512]{1,0:T(8,128)(2,1)}, bf16[128,512]{1,0:T(8,128)(2,1)S(1)}, u32[]{:S(2)}, u32[]{:S(2)}) %collective-permute-start.17) | collective-permute-done | bytes 131104 | tf_op jit(solution)/shard_map/ppermute | solution.py:21
  111.5 0.0 copy-done.4
  111.6 0.6 copy-done.8
  112.2 6.0 %node.3 = bf16[1024,512]{1,0:T(8,128)(2,1)} custom-call(s32[4]{0:T(128)} %bitcast.27, bf16[128,512]{1,0:T(8,128)(2,1)} %copy-done.2, bf16[128,512]{1,0:T(8,128)(2,1)} %copy-done.4, bf16[128,512]{1,0:T(8,128)(2,1)} %copy-done.6, bf16[128,512]{1,0:T(8,128)(2,1)} %copy-done.8, f32[1024,512]{1,0:T(8,128)} %get-tuple-element.60.own, f32[1024,512]{1,0:T(8,128)} %ready.3.partial, ...), custom_call_target="tpu_custom_call" | custom-call | flops 1073741824 | bytes 8388608 | tf_op jit(solution)/shard_map/node/pallas_call | solution.py:40
  (20 shorter events, 0.0 us)
Async XLA Ops:
  2.7 15.5 %collective-permute-start = (bf16[128,512]{1,0:T(8,128)(2,1)}, bf16[128,512]{1,0:T(8,128)(2,1)S(1)}, u32[]{:S(2)}, u32[]{:S(2)}) collective-permute-start(bf16[128,512]{1,0:T(8,128)(2,1)} %get-tuple-element.32), channel_id=1, source_target_pairs={{7,0},{0,1},{1,2},{2,3},{3,4},{4,5},{5,6},{6,7},{15,8},{8,9},{9,10... | collective-permute-start | bytes 393224 | tf_op jit(solution)/shard_map/ppermute | solution.py:21
  4.2 14.0 %collective-permute-start.1 = (bf16[128,512]{1,0:T(8,128)(2,1)}, bf16[128,512]{1,0:T(8,128)(2,1)S(1)}, u32[]{:S(2)}, u32[]{:S(2)}) collective-permute-start(bf16[128,512]{1,0:T(8,128)(2,1)} %get-tuple-element.33), channel_id=1, source_target_pairs={{1,0},{2,1},{3,2},{4,3},{5,4},{6,5},{7,6},{0,7},{9,8},{10,9},{11,1... | collective-permute-start | bytes 393224 | tf_op jit(solution)/shard_map/ppermute | solution.py:21
  4.7 13.5 %collective-permute-start.2 = (bf16[128,512]{1,0:T(8,128)(2,1)}, bf16[128,512]{1,0:T(8,128)(2,1)S(1)}, u32[]{:S(2)}, u32[]{:S(2)}) collective-permute-start(bf16[128,512]{1,0:T(8,128)(2,1)} %get-tuple-element.34), channel_id=1, source_target_pairs={{6,0},{7,1},{0,2},{1,3},{2,4},{3,5},{4,6},{5,7},{14,8},{15,9},{8,1... | collective-permute-start | bytes 393224 | tf_op jit(solution)/shard_map/ppermute | solution.py:21
  6.3 11.9 %collective-permute-start.3 = (bf16[128,512]{1,0:T(8,128)(2,1)}, bf16[128,512]{1,0:T(8,128)(2,1)S(1)}, u32[]{:S(2)}, u32[]{:S(2)}) collective-permute-start(bf16[128,512]{1,0:T(8,128)(2,1)} %get-tuple-element.35), channel_id=1, source_target_pairs={{2,0},{3,1},{4,2},{5,3},{6,4},{7,5},{0,6},{1,7},{10,8},{11,9},{12,... | collective-permute-start | bytes 393224 | tf_op jit(solution)/shard_map/ppermute | solution.py:21
  18.2 0.7 copy-start.12
  18.2 0.7 copy-start.14
  18.2 0.7 copy-start.16
  18.2 0.8 copy-start.17
  29.3 48.2 %collective-permute-start.13 = (bf16[1536,512]{1,0:T(8,128)(2,1)}, bf16[1536,512]{1,0:T(8,128)(2,1)S(1)}, u32[]{:S(2)}, u32[]{:S(2)}) collective-permute-start(bf16[1536,512]{1,0:T(8,128)(2,1)} %get-tuple-element.50), channel_id=1, source_target_pairs={{0,8},{8,16},{16,24},{1,9},{9,17},{17,25},{2,10},{10,18},{18,26},{... | collective-permute-start | bytes 4718600 | tf_op jit(solution)/shard_map/ppermute | solution.py:26
  31.3 10.2 %collective-permute-start.4 = (bf16[128,512]{1,0:T(8,128)(2,1)}, bf16[128,512]{1,0:T(8,128)(2,1)S(1)}, u32[]{:S(2)}, u32[]{:S(2)}) collective-permute-start(bf16[128,512]{1,0:T(8,128)(2,1)} %get-tuple-element.41), channel_id=1, source_target_pairs={{1,0},{2,1},{3,2},{4,3},{5,4},{6,5},{7,6},{0,7},{9,8},{10,9},{11,1... | collective-permute-start | bytes 393224 | tf_op jit(solution)/shard_map/ppermute | solution.py:21
  34.5 7.0 %collective-permute-start.5 = (bf16[128,512]{1,0:T(8,128)(2,1)}, bf16[128,512]{1,0:T(8,128)(2,1)S(1)}, u32[]{:S(2)}, u32[]{:S(2)}) collective-permute-start(bf16[128,512]{1,0:T(8,128)(2,1)} %get-tuple-element.42), channel_id=1, source_target_pairs={{7,0},{0,1},{1,2},{2,3},{3,4},{4,5},{5,6},{6,7},{15,8},{8,9},{9,10... | collective-permute-start | bytes 393224 | tf_op jit(solution)/shard_map/ppermute | solution.py:21
  34.5 7.0 %collective-permute-start.6 = (bf16[128,512]{1,0:T(8,128)(2,1)}, bf16[128,512]{1,0:T(8,128)(2,1)S(1)}, u32[]{:S(2)}, u32[]{:S(2)}) collective-permute-start(bf16[128,512]{1,0:T(8,128)(2,1)} %get-tuple-element.43), channel_id=1, source_target_pairs={{2,0},{3,1},{4,2},{5,3},{6,4},{7,5},{0,6},{1,7},{10,8},{11,9},{12,... | collective-permute-start | bytes 393224 | tf_op jit(solution)/shard_map/ppermute | solution.py:21
  37.8 7.4 %collective-permute-start.7 = (bf16[128,512]{1,0:T(8,128)(2,1)}, bf16[128,512]{1,0:T(8,128)(2,1)S(1)}, u32[]{:S(2)}, u32[]{:S(2)}) collective-permute-start(bf16[128,512]{1,0:T(8,128)(2,1)} %get-tuple-element.44), channel_id=1, source_target_pairs={{6,0},{7,1},{0,2},{1,3},{2,4},{3,5},{4,6},{5,7},{14,8},{15,9},{8,1... | collective-permute-start | bytes 393224 | tf_op jit(solution)/shard_map/ppermute | solution.py:21
  41.5 3.8 %copy-start.1 = (bf16[128,512]{1,0:T(8,128)(2,1)}, bf16[128,512]{1,0:T(8,128)(2,1)S(1)}, u32[]{:S(2)}) copy-start(bf16[128,512]{1,0:T(8,128)(2,1)S(1)} %collective-permute-done.4.back_one) | copy-start | bytes 393220
  41.5 3.8 %copy-start.3 = (bf16[128,512]{1,0:T(8,128)(2,1)}, bf16[128,512]{1,0:T(8,128)(2,1)S(1)}, u32[]{:S(2)}) copy-start(bf16[128,512]{1,0:T(8,128)(2,1)S(1)} %collective-permute-done.5.back_two) | copy-start | bytes 393220
  41.5 3.7 %copy-start.5 = (bf16[128,512]{1,0:T(8,128)(2,1)}, bf16[128,512]{1,0:T(8,128)(2,1)S(1)}, u32[]{:S(2)}) copy-start(bf16[128,512]{1,0:T(8,128)(2,1)S(1)} %collective-permute-done.6.back_three) | copy-start | bytes 393220
  45.3 0.7 copy-start.7
  52.0 16.8 %collective-permute-start.8 = (bf16[1024,512]{1,0:T(8,128)(2,1)}, bf16[1024,512]{1,0:T(8,128)(2,1)S(1)}, u32[]{:S(2)}, u32[]{:S(2)}) collective-permute-start(bf16[1024,512]{1,0:T(8,128)(2,1)} %node.2), channel_id=1, source_target_pairs={{0,8},{8,16},{16,24},{1,9},{9,17},{17,25},{2,10},{10,18},{18,26},{... | collective-permute-start | bytes 3145736 | tf_op jit(solution)/shard_map/ppermute | solution.py:26
  68.8 1.0 copy-start
  72.6 12.5 %collective-permute-start.10 = (bf16[128,512]{1,0:T(8,128)(2,1)}, bf16[128,512]{1,0:T(8,128)(2,1)S(1)}, u32[]{:S(2)}, u32[]{:S(2)}) collective-permute-start(bf16[128,512]{1,0:T(8,128)(2,1)} %get-tuple-element.47), channel_id=1, source_target_pairs={{1,0},{2,1},{3,2},{4,3},{5,4},{6,5},{7,6},{0,7},{9,8},{10,9},{11,1... | collective-permute-start | bytes 393224 | tf_op jit(solution)/shard_map/ppermute | solution.py:21
  72.6 12.5 %collective-permute-start.11 = (bf16[128,512]{1,0:T(8,128)(2,1)}, bf16[128,512]{1,0:T(8,128)(2,1)S(1)}, u32[]{:S(2)}, u32[]{:S(2)}) collective-permute-start(bf16[128,512]{1,0:T(8,128)(2,1)} %get-tuple-element.48), channel_id=1, source_target_pairs={{6,0},{7,1},{0,2},{1,3},{2,4},{3,5},{4,6},{5,7},{14,8},{15,9},{8,1... | collective-permute-start | bytes 393224 | tf_op jit(solution)/shard_map/ppermute | solution.py:21
  72.6 12.5 %collective-permute-start.12 = (bf16[128,512]{1,0:T(8,128)(2,1)}, bf16[128,512]{1,0:T(8,128)(2,1)S(1)}, u32[]{:S(2)}, u32[]{:S(2)}) collective-permute-start(bf16[128,512]{1,0:T(8,128)(2,1)} %get-tuple-element.49), channel_id=1, source_target_pairs={{2,0},{3,1},{4,2},{5,3},{6,4},{7,5},{0,6},{1,7},{10,8},{11,9},{12,... | collective-permute-start | bytes 393224 | tf_op jit(solution)/shard_map/ppermute | solution.py:21
  76.4 8.7 %collective-permute-start.9 = (bf16[128,512]{1,0:T(8,128)(2,1)}, bf16[128,512]{1,0:T(8,128)(2,1)S(1)}, u32[]{:S(2)}, u32[]{:S(2)}) collective-permute-start(bf16[128,512]{1,0:T(8,128)(2,1)} %get-tuple-element.46), channel_id=1, source_target_pairs={{7,0},{0,1},{1,2},{2,3},{3,4},{4,5},{5,6},{6,7},{15,8},{8,9},{9,10... | collective-permute-start | bytes 393224 | tf_op jit(solution)/shard_map/ppermute | solution.py:21
  77.6 1.1 copy-start.9
  85.1 0.7 copy-start.10
  85.1 0.7 copy-start.11
  85.1 0.7 copy-start.13
  85.1 0.8 copy-start.15
  96.2 12.0 %collective-permute-start.14 = (bf16[128,512]{1,0:T(8,128)(2,1)}, bf16[128,512]{1,0:T(8,128)(2,1)S(1)}, u32[]{:S(2)}, u32[]{:S(2)}) collective-permute-start(bf16[128,512]{1,0:T(8,128)(2,1)} %get-tuple-element.56), channel_id=1, source_target_pairs={{1,0},{2,1},{3,2},{4,3},{5,4},{6,5},{7,6},{0,7},{9,8},{10,9},{11,1... | collective-permute-start | bytes 393224 | tf_op jit(solution)/shard_map/ppermute | solution.py:21
  97.1 11.1 %collective-permute-start.15 = (bf16[128,512]{1,0:T(8,128)(2,1)}, bf16[128,512]{1,0:T(8,128)(2,1)S(1)}, u32[]{:S(2)}, u32[]{:S(2)}) collective-permute-start(bf16[128,512]{1,0:T(8,128)(2,1)} %get-tuple-element.57), channel_id=1, source_target_pairs={{7,0},{0,1},{1,2},{2,3},{3,4},{4,5},{5,6},{6,7},{15,8},{8,9},{9,10... | collective-permute-start | bytes 393224 | tf_op jit(solution)/shard_map/ppermute | solution.py:21
  99.1 9.1 %collective-permute-start.16 = (bf16[128,512]{1,0:T(8,128)(2,1)}, bf16[128,512]{1,0:T(8,128)(2,1)S(1)}, u32[]{:S(2)}, u32[]{:S(2)}) collective-permute-start(bf16[128,512]{1,0:T(8,128)(2,1)} %get-tuple-element.58), channel_id=1, source_target_pairs={{2,0},{3,1},{4,2},{5,3},{6,4},{7,5},{0,6},{1,7},{10,8},{11,9},{12,... | collective-permute-start | bytes 393224 | tf_op jit(solution)/shard_map/ppermute | solution.py:21
  104.6 7.0 %collective-permute-start.17 = (bf16[128,512]{1,0:T(8,128)(2,1)}, bf16[128,512]{1,0:T(8,128)(2,1)S(1)}, u32[]{:S(2)}, u32[]{:S(2)}) collective-permute-start(bf16[128,512]{1,0:T(8,128)(2,1)} %get-tuple-element.59), channel_id=1, source_target_pairs={{6,0},{7,1},{0,2},{1,3},{2,4},{3,5},{4,6},{5,7},{14,8},{15,9},{8,1... | collective-permute-start | bytes 393224 | tf_op jit(solution)/shard_map/ppermute | solution.py:21
  108.2 3.4 %copy-start.2 = (bf16[128,512]{1,0:T(8,128)(2,1)}, bf16[128,512]{1,0:T(8,128)(2,1)S(1)}, u32[]{:S(2)}) copy-start(bf16[128,512]{1,0:T(8,128)(2,1)S(1)} %collective-permute-done.14.back_one) | copy-start | bytes 393220
  108.2 3.4 %copy-start.4 = (bf16[128,512]{1,0:T(8,128)(2,1)}, bf16[128,512]{1,0:T(8,128)(2,1)S(1)}, u32[]{:S(2)}) copy-start(bf16[128,512]{1,0:T(8,128)(2,1)S(1)} %collective-permute-done.15.back_two) | copy-start | bytes 393220
  108.2 3.3 %copy-start.6 = (bf16[128,512]{1,0:T(8,128)(2,1)}, bf16[128,512]{1,0:T(8,128)(2,1)S(1)}, u32[]{:S(2)}) copy-start(bf16[128,512]{1,0:T(8,128)(2,1)S(1)} %collective-permute-done.16.back_three) | copy-start | bytes 393220
  111.5 0.7 copy-start.8
where the time goes:
time: 119 us; the launch traced here: 118 us
  Pallas kernels  59.5 us (50%)
  starting transfers between devices  29.6 us (25%)
  waiting for transfers between devices  22 us (18%)
  local copies, waits for them, and re-layouts  6.32 us (5%)
    pallas_call x11, Pallas kernels, call(): pl.pallas_call(kernel, name=name, out_shape=outs, in_specs=ins, out_specs...  59.5 us
    ppermute x16, starting transfers between devices, passed_along(): return lax.ppermute(block, axis, route)  25.7 us
    ppermute x2, waiting for transfers between devices, from_behind(): lax.ppermute(value, axis, [(source, source + 1) for source in range(count...  14.9 us
    ppermute x16, waiting for transfers between devices, passed_along(): return lax.ppermute(block, axis, route)  7.13 us
    unnamed x36, local copies, waits for them, and re-layouts  4.96 us
    ppermute x2, starting transfers between devices, from_behind(): lax.ppermute(value, axis, [(source, source + 1) for source in range(count...  3.82 us
  transfers between devices with their start and end apart: 18, of which 4 were waited for; matrix products, arithmetic and copies ran while one was open for 1% of the time, Pallas kernels for 26%

commit v1 on v0

--- a/solution.py
+++ b/solution.py
@@ -44,7 +44,7 @@
         in_specs=ins,
         out_specs=jax.tree.map(lambda _: VMEM, outs),
         scratch_shapes=list(scratch),
-        compiler_params=pltpu.CompilerParams(vmem_limit_bytes=60 << 20),
+        compiler_params=pltpu.CompilerParams(vmem_limit_bytes=24 << 20),
         cost_estimate=pl.CostEstimate(flops=flops, bytes_accessed=moved, transcendentals=0),
     )(*operands)
 

time: 119 us -> 97.6 us (0.82)
  Pallas kernels: 59.5 us -> 27.9 us
  waiting for transfers between devices: 22 us -> 28.8 us
  local copies, waits for them, and re-layouts: 6.32 us -> 10.4 us
    pallas_call x11, Pallas kernels: 59.5 us -> 27.9 us  [call(): pl.pallas_call(kernel, name=name, out_shape=outs, in_specs=ins, out_specs...]
    ppermute x16, waiting for transfers between devices: 7.13 us -> 12.8 us  [passed_along(): return lax.ppermute(block, axis, route)]
    unnamed x36 -> x40, local copies, waits for them, and re-layouts: 4.96 us -> 9.62 us
  transfers between devices with their start and end apart: 18 -> 18, of which waited for: 4 -> 7; matrix products, arithmetic and copies ran while one was open for 1% -> 1% of each run, Pallas kernels for 26% -> 12%
where the time goes in v1:
time: 97.6 us; the launch traced here: 97.2 us
  starting transfers between devices  29.2 us (30%)
  waiting for transfers between devices  28.8 us (30%)
  Pallas kernels  27.9 us (29%)
  local copies, waits for them, and re-layouts  10.4 us (11%)
    pallas_call x11, Pallas kernels, call(): pl.pallas_call(kernel, name=name, out_shape=outs, in_specs=ins, out_specs...  27.9 us
    ppermute x16, starting transfers between devices, passed_along(): return lax.ppermute(block, axis, route)  25.3 us
    ppermute x2, waiting for transfers between devices, from_behind(): lax.ppermute(value, axis, [(source, source + 1) for source in range(count...  16 us
    ppermute x16, waiting for transfers between devices, passed_along(): return lax.ppermute(block, axis, route)  12.8 us
    unnamed x40, local copies, waits for them, and re-layouts  9.62 us
    ppermute x2, starting transfers between devices, from_behind(): lax.ppermute(value, axis, [(source, source + 1) for source in range(count...  3.82 us
  transfers between devices with their start and end apart: 18, of which 7 were waited for; matrix products, arithmetic and copies ran while one was open for 1% of the time, Pallas kernels for 12%

profile of v1, /device:TPU:6, one launch (start us, length us, event | category | flops | bytes accessed | tf_op | source)
XLA Modules:
  0.0 97.2 jit_solution(12748547909724779358)
XLA Ops:
  0.6 0.0 copy-start.1
  0.6 1.2 %copy-done.1 = bf16[1,1024,512]{2,1,0:T(8,128)(2,1)S(1)} copy-done((bf16[1,1024,512]{2,1,0:T(8,128)(2,1)S(1)}, bf16[1,1024,512]{2,1,0:T(8,128)(2,1)}, u32[]{:S(2)}) %copy-start.1) | copy-done | bytes 1048600
  1.9 0.7 copy-done.8
  2.5 0.6 pick.1
  3.1 1.6 %collective-permute-start = (bf16[128,512]{1,0:T(8,128)(2,1)S(1)}, bf16[128,512]{1,0:T(8,128)(2,1)S(1)}, u32[]{:S(2)}, u32[]{:S(2)}) collective-permute-start(bf16[128,512]{1,0:T(8,128)(2,1)S(1)} %get-tuple-element.32), channel_id=1, source_target_pairs={{7,0},{0,1},{1,2},{2,3},{3,4},{4,5},{5,6},{6,7},{15,8},{8,9},{9,10... | collective-permute-start | bytes 393224 | tf_op jit(solution)/shard_map/ppermute | solution.py:21
  4.7 0.5 collective-permute-start.1
  5.2 1.6 %collective-permute-start.2 = (bf16[128,512]{1,0:T(8,128)(2,1)S(1)}, bf16[128,512]{1,0:T(8,128)(2,1)S(1)}, u32[]{:S(2)}, u32[]{:S(2)}) collective-permute-start(bf16[128,512]{1,0:T(8,128)(2,1)S(1)} %get-tuple-element.34), channel_id=1, source_target_pairs={{6,0},{7,1},{0,2},{1,3},{2,4},{3,5},{4,6},{5,7},{14,8},{15,9},{8,1... | collective-permute-start | bytes 393224 | tf_op jit(solution)/shard_map/ppermute | solution.py:21
  6.8 2.2 %collective-permute-start.3 = (bf16[128,512]{1,0:T(8,128)(2,1)S(1)}, bf16[128,512]{1,0:T(8,128)(2,1)S(1)}, u32[]{:S(2)}, u32[]{:S(2)}) collective-permute-start(bf16[128,512]{1,0:T(8,128)(2,1)S(1)} %get-tuple-element.35), channel_id=1, source_target_pairs={{2,0},{3,1},{4,2},{5,3},{6,4},{7,5},{0,6},{1,7},{10,8},{11,9},{12,... | collective-permute-start | bytes 393224 | tf_op jit(solution)/shard_map/ppermute | solution.py:21
  9.0 0.8 copy.18
  9.8 1.1 %copy-done.5 = s32[1536,128]{1,0:T(8,128)S(1)} copy-done((s32[1536,128]{1,0:T(8,128)S(1)}, s32[1536,128]{1,0:T(8,128)}, u32[]{:S(2)}) %copy-start.5) | copy-done | bytes 786456
  10.9 1.1 %copy-done.6 = s32[1536,128]{1,0:T(8,128)S(1)} copy-done((s32[1536,128]{1,0:T(8,128)S(1)}, s32[1536,128]{1,0:T(8,128)}, u32[]{:S(2)}) %copy-start.6) | copy-done | bytes 786456
  12.0 0.3 ends.1
  12.3 0.0 copy-start.14
  12.3 0.0 copy-done.2
  12.3 1.4 %copy-done.10 = bf16[1,1536,512]{2,1,0:T(8,128)(2,1)S(1)} copy-done((bf16[1,1536,512]{2,1,0:T(8,128)(2,1)S(1)}, bf16[1,1536,512]{2,1,0:T(8,128)(2,1)}, u32[]{:S(2)}) %copy-start.10) | copy-done | bytes 1572888
  13.7 1.4 %copy-done.12 = bf16[1,1536,512]{2,1,0:T(8,128)(2,1)S(1)} copy-done((bf16[1,1536,512]{2,1,0:T(8,128)(2,1)S(1)}, bf16[1,1536,512]{2,1,0:T(8,128)(2,1)}, u32[]{:S(2)}) %copy-start.12) | copy-done | bytes 1572888
  15.1 2.1 %project.1 = (f32[1536,512]{1,0:T(8,128)S(1)}, bf16[1024,512]{1,0:T(8,128)(2,1)S(1)}, bf16[1024,512]{1,0:T(8,128)(2,1)S(1)}) custom-call(bf16[1536,512]{1,0:T(8,128)(2,1)S(1)} %bitcast.27, bf16[1024,512]{1,0:T(8,128)(2,1)S(1)} %bitcast.16, bf16[1536,512]{1,0:T(8,128)(2,1)S(1)} %bitcast.29), custom_call_target="tpu_custom_call" | custom-call | flops 1879048192 | bytes 9437184 | tf_op jit(solution)/shard_map/project/pallas_call | solution.py:40
  17.2 0.0 collective-permute-done.in_one
  17.2 0.0 collective-permute-done.1.in_two
  17.2 0.0 collective-permute-done.2.in_three
  17.3 0.0 collective-permute-done.3.in_four
  17.3 0.0 copy-done.14
  17.3 0.0 copy-start
  17.3 6.0 %edge.2 = (bf16[1536,512]{1,0:T(8,128)(2,1)}, f32[1024,512]{1,0:T(8,128)S(1)}, bf16[128,512]{1,0:T(8,128)(2,1)S(1)}, bf16[128,512]{1,0:T(8,128)(2,1)S(1)}, bf16[...) custom-call(s32[12,3]{1,0:T(8,128)S(1)} %bitcast.21, bf16[128,512]{1,0:T(8,128)(2,1)S(1)} %collective-permute-done.in_one, ...), custom_call_target="tpu_custom_call" | custom-call | flops 4000000000 | bytes 12582912 | tf_op jit(solution)/shard_map/edge/pallas_call | solution.py:40
  23.3 1.9 %collective-permute-start.13 = (bf16[1536,512]{1,0:T(8,128)(2,1)}, bf16[1536,512]{1,0:T(8,128)(2,1)}, u32[]{:S(2)}, u32[]{:S(2)}) collective-permute-start(bf16[1536,512]{1,0:T(8,128)(2,1)} %get-tuple-element.50), channel_id=1, source_target_pairs={{0,8},{8,16},{16,24},{1,9},{9,17},{17,25},{2,10},{10,18},{18,26},{... | collective-permute-start | bytes 4718600 | tf_op jit(solution)/shard_map/ppermute | solution.py:26
  25.2 3.3 %collective-permute-start.4 = (bf16[128,512]{1,0:T(8,128)(2,1)S(1)}, bf16[128,512]{1,0:T(8,128)(2,1)S(1)}, u32[]{:S(2)}, u32[]{:S(2)}) collective-permute-start(bf16[128,512]{1,0:T(8,128)(2,1)S(1)} %get-tuple-element.41), channel_id=1, source_target_pairs={{1,0},{2,1},{3,2},{4,3},{5,4},{6,5},{7,6},{0,7},{9,8},{10,9},{11,1... | collective-permute-start | bytes 393224 | tf_op jit(solution)/shard_map/ppermute | solution.py:21
  28.5 0.0 collective-permute-start.5
  28.5 3.3 %collective-permute-start.6 = (bf16[128,512]{1,0:T(8,128)(2,1)S(1)}, bf16[128,512]{1,0:T(8,128)(2,1)S(1)}, u32[]{:S(2)}, u32[]{:S(2)}) collective-permute-start(bf16[128,512]{1,0:T(8,128)(2,1)S(1)} %get-tuple-element.43), channel_id=1, source_target_pairs={{2,0},{3,1},{4,2},{5,3},{6,4},{7,5},{0,6},{1,7},{10,8},{11,9},{12,... | collective-permute-start | bytes 393224 | tf_op jit(solution)/shard_map/ppermute | solution.py:21
  31.8 0.0 collective-permute-start.7
  31.8 0.0 copy-start.9
  31.9 0.7 ready.2.partial
  32.6 0.0 collective-permute-done.4.back_one
  32.6 0.9 collective-permute-done.5.back_two
  33.5 1.7 %collective-permute-done.6.back_three = bf16[128,512]{1,0:T(8,128)(2,1)S(1)} collective-permute-done((bf16[128,512]{1,0:T(8,128)(2,1)S(1)}, bf16[128,512]{1,0:T(8,128)(2,1)S(1)}, u32[]{:S(2)}, u32[]{:S(2)}) %collective-permute-start.6) | collective-permute-done | bytes 131104 | tf_op jit(solution)/shard_map/ppermute | solution.py:21
  35.2 3.9 %collective-permute-done.7.back_four = bf16[128,512]{1,0:T(8,128)(2,1)S(1)} collective-permute-done((bf16[128,512]{1,0:T(8,128)(2,1)S(1)}, bf16[128,512]{1,0:T(8,128)(2,1)S(1)}, u32[]{:S(2)}, u32[]{:S(2)}) %collective-permute-start.7) | collective-permute-done | bytes 131104 | tf_op jit(solution)/shard_map/ppermute | solution.py:21
  39.1 0.0 copy-done.7
  39.1 3.5 %node.2 = bf16[1024,512]{1,0:T(8,128)(2,1)} custom-call(s32[4]{0:T(128)S(1)} %bitcast.24, bf16[128,512]{1,0:T(8,128)(2,1)S(1)} %collective-permute-done.4.back_one, bf16[128,512]{1,0:T(8,128)(2,1)S(1)} %collective-permute-done.5.back_two, bf16[128,512]{1,0:T(8,128)(2,1)S(1)} %collective-permute-done.6.back_three, ...), custom_call_target="tpu_custom_call" | custom-call | flops 1073741824 | bytes 8388608 | tf_op jit(solution)/shard_map/node/pallas_call | solution.py:40
  42.6 1.9 %collective-permute-start.8 = (bf16[1024,512]{1,0:T(8,128)(2,1)}, bf16[1024,512]{1,0:T(8,128)(2,1)S(1)}, u32[]{:S(2)}, u32[]{:S(2)}) collective-permute-start(bf16[1024,512]{1,0:T(8,128)(2,1)} %node.2), channel_id=1, source_target_pairs={{0,8},{8,16},{16,24},{1,9},{9,17},{17,25},{2,10},{10,18},{18,26},{... | collective-permute-start | bytes 3145736 | tf_op jit(solution)/shard_map/ppermute | solution.py:26
  44.5 16.0 %collective-permute-done.8.moved = bf16[1024,512]{1,0:T(8,128)(2,1)S(1)} collective-permute-done((bf16[1024,512]{1,0:T(8,128)(2,1)}, bf16[1024,512]{1,0:T(8,128)(2,1)S(1)}, u32[]{:S(2)}, u32[]{:S(2)}) %collective-permute-start.8) | collective-permute-done | bytes 1048608 | tf_op jit(solution)/shard_map/ppermute | solution.py:26
  60.5 1.2 %copy-done.4 = bf16[1024,512]{1,0:T(8,128)(2,1)S(1)} copy-done((bf16[1024,512]{1,0:T(8,128)(2,1)S(1)}, bf16[1024,512]{1,0:T(8,128)(2,1)}, u32[]{:S(2)}) %copy-start.4) | copy-done | bytes 1048600
  61.7 0.7 pick_select.1
  62.4 0.1 collective-permute-start.10
  62.4 0.1 collective-permute-start.11
  62.5 3.8 %collective-permute-start.12 = (bf16[128,512]{1,0:T(8,128)(2,1)S(1)}, bf16[128,512]{1,0:T(8,128)(2,1)S(1)}, u32[]{:S(2)}, u32[]{:S(2)}) collective-permute-start(bf16[128,512]{1,0:T(8,128)(2,1)S(1)} %get-tuple-element.49), channel_id=1, source_target_pairs={{2,0},{3,1},{4,2},{5,3},{6,4},{7,5},{0,6},{1,7},{10,8},{11,9},{12,... | collective-permute-start | bytes 393224 | tf_op jit(solution)/shard_map/ppermute | solution.py:21
  66.3 1.1 %collective-permute-start.9 = (bf16[128,512]{1,0:T(8,128)(2,1)S(1)}, bf16[128,512]{1,0:T(8,128)(2,1)S(1)}, u32[]{:S(2)}, u32[]{:S(2)}) collective-permute-start(bf16[128,512]{1,0:T(8,128)(2,1)S(1)} %get-tuple-element.46), channel_id=1, source_target_pairs={{7,0},{0,1},{1,2},{2,3},{3,4},{4,5},{5,6},{6,7},{15,8},{8,9},{9,10... | collective-permute-start | bytes 393224 | tf_op jit(solution)/shard_map/ppermute | solution.py:21
  67.4 0.0 collective-permute-done.13.moved
  67.4 1.4 %copy-done.13 = bf16[1,1536,512]{2,1,0:T(8,128)(2,1)S(1)} copy-done((bf16[1,1536,512]{2,1,0:T(8,128)(2,1)S(1)}, bf16[1,1536,512]{2,1,0:T(8,128)(2,1)}, u32[]{:S(2)}) %copy-start.13) | copy-done | bytes 1572888
  68.8 3.9 %project_select.1 = (bf16[1536,512]{1,0:T(8,128)(2,1)S(1)}, f32[1536,512]{1,0:T(8,128)S(1)}, bf16[1024,512]{1,0:T(8,128)(2,1)S(1)}, bf16[1024,512]{1,0:T(8,128)(2,1)S(1)}) custom-call(s32[1]{0:T(128)} %bitcast.2.flag, bf16[1536,512]{1,0:T(8,128)(2,1)S(1)} %copy-done.11, bf16[1536,512]{1,0:T(8,128)(2,1)} %collective-permute-done.13.moved, ...), custom_call_target="tpu_custom_call" | custom-call | flops 1879048192 | bytes 9437184 | tf_op jit(solution)/shard_map/project_select/pallas_call | solution.py:40
  72.7 0.0 collective-permute-done.10.in_two
  72.7 0.0 collective-permute-done.11.in_three
  72.7 0.0 collective-permute-done.12.in_four
  72.7 0.3 collective-permute-done.9.in_one
  72.9 0.0 copy-done.17
  73.0 6.1 %edge.3 = (bf16[1536,512]{1,0:T(8,128)(2,1)}, f32[1024,512]{1,0:T(8,128)S(1)}, bf16[128,512]{1,0:T(8,128)(2,1)S(1)}, bf16[128,512]{1,0:T(8,128)(2,1)S(1)}, bf16[...) custom-call(s32[12,3]{1,0:T(8,128)S(1)} %bitcast.22, bf16[128,512]{1,0:T(8,128)(2,1)S(1)} %collective-permute-done.9.in_one, ...), custom_call_target="tpu_custom_call" | custom-call | flops 4000000000 | bytes 12582912 | tf_op jit(solution)/shard_map/edge/pallas_call | solution.py:40
  79.0 2.3 %collective-permute-start.14 = (bf16[128,512]{1,0:T(8,128)(2,1)S(1)}, bf16[128,512]{1,0:T(8,128)(2,1)S(1)}, u32[]{:S(2)}, u32[]{:S(2)}) collective-permute-start(bf16[128,512]{1,0:T(8,128)(2,1)S(1)} %get-tuple-element.56), channel_id=1, source_target_pairs={{1,0},{2,1},{3,2},{4,3},{5,4},{6,5},{7,6},{0,7},{9,8},{10,9},{11,1... | collective-permute-start | bytes 393224 | tf_op jit(solution)/shard_map/ppermute | solution.py:21
  81.3 0.6 collective-permute-start.15
  82.0 4.9 %collective-permute-start.16 = (bf16[128,512]{1,0:T(8,128)(2,1)S(1)}, bf16[128,512]{1,0:T(8,128)(2,1)S(1)}, u32[]{:S(2)}, u32[]{:S(2)}) collective-permute-start(bf16[128,512]{1,0:T(8,128)(2,1)S(1)} %get-tuple-element.58), channel_id=1, source_target_pairs={{2,0},{3,1},{4,2},{5,3},{6,4},{7,5},{0,6},{1,7},{10,8},{11,9},{12,... | collective-permute-start | bytes 393224 | tf_op jit(solution)/shard_map/ppermute | solution.py:21
  86.9 0.0 collective-permute-start.17
  86.9 0.7 ready.3.partial
  87.6 0.0 collective-permute-done.14.back_one
  87.6 0.0 collective-permute-done.15.back_two
  87.6 1.8 %collective-permute-done.16.back_three = bf16[128,512]{1,0:T(8,128)(2,1)S(1)} collective-permute-done((bf16[128,512]{1,0:T(8,128)(2,1)S(1)}, bf16[128,512]{1,0:T(8,128)(2,1)S(1)}, u32[]{:S(2)}, u32[]{:S(2)}) %collective-permute-start.16) | collective-permute-done | bytes 131104 | tf_op jit(solution)/shard_map/ppermute | solution.py:21
  89.4 4.2 %collective-permute-done.17.back_four = bf16[128,512]{1,0:T(8,128)(2,1)S(1)} collective-permute-done((bf16[128,512]{1,0:T(8,128)(2,1)S(1)}, bf16[128,512]{1,0:T(8,128)(2,1)S(1)}, u32[]{:S(2)}, u32[]{:S(2)}) %collective-permute-start.17) | collective-permute-done | bytes 131104 | tf_op jit(solution)/shard_map/ppermute | solution.py:21
  93.7 3.5 %node.3 = bf16[1024,512]{1,0:T(8,128)(2,1)} custom-call(s32[4]{0:T(128)S(1)} %bitcast.26, bf16[128,512]{1,0:T(8,128)(2,1)S(1)} %collective-permute-done.14.back_one, bf16[128,512]{1,0:T(8,128)(2,1)S(1)} %collective-permute-done.15.back_two, bf16[128,512]{1,0:T(8,128)(2,1)S(1)} %collective-permute-done.16.back_three, ...), custom_call_target="tpu_custom_call" | custom-call | flops 1073741824 | bytes 8388608 | tf_op jit(solution)/shard_map/node/pallas_call | solution.py:40
  (24 shorter events, 0.0 us)
Async XLA Ops:
  0.6 1.2 %copy-start.1 = (bf16[1,1024,512]{2,1,0:T(8,128)(2,1)S(1)}, bf16[1,1024,512]{2,1,0:T(8,128)(2,1)}, u32[]{:S(2)}) copy-start(bf16[1,1024,512]{2,1,0:T(8,128)(2,1)} %param.14) | copy-start | bytes 3145732
  1.9 0.7 copy-start.8
  2.5 9.8 %copy-start.2 = (bf16[1,1024,512]{2,1,0:T(8,128)(2,1)S(1)}, bf16[1,1024,512]{2,1,0:T(8,128)(2,1)}, u32[]{:S(2)}) copy-start(bf16[1,1024,512]{2,1,0:T(8,128)(2,1)} %param.14) | copy-start | bytes 3145732
  3.1 14.1 %collective-permute-start = (bf16[128,512]{1,0:T(8,128)(2,1)S(1)}, bf16[128,512]{1,0:T(8,128)(2,1)S(1)}, u32[]{:S(2)}, u32[]{:S(2)}) collective-permute-start(bf16[128,512]{1,0:T(8,128)(2,1)S(1)} %get-tuple-element.32), channel_id=1, source_target_pairs={{7,0},{0,1},{1,2},{2,3},{3,4},{4,5},{5,6},{6,7},{15,8},{8,9},{9,10... | collective-permute-start | bytes 393224 | tf_op jit(solution)/shard_map/ppermute | solution.py:21
  4.7 12.6 %collective-permute-start.1 = (bf16[128,512]{1,0:T(8,128)(2,1)S(1)}, bf16[128,512]{1,0:T(8,128)(2,1)S(1)}, u32[]{:S(2)}, u32[]{:S(2)}) collective-permute-start(bf16[128,512]{1,0:T(8,128)(2,1)S(1)} %get-tuple-element.33), channel_id=1, source_target_pairs={{1,0},{2,1},{3,2},{4,3},{5,4},{6,5},{7,6},{0,7},{9,8},{10,9},{11,1... | collective-permute-start | bytes 393224 | tf_op jit(solution)/shard_map/ppermute | solution.py:21
  5.2 12.1 %collective-permute-start.2 = (bf16[128,512]{1,0:T(8,128)(2,1)S(1)}, bf16[128,512]{1,0:T(8,128)(2,1)S(1)}, u32[]{:S(2)}, u32[]{:S(2)}) collective-permute-start(bf16[128,512]{1,0:T(8,128)(2,1)S(1)} %get-tuple-element.34), channel_id=1, source_target_pairs={{6,0},{7,1},{0,2},{1,3},{2,4},{3,5},{4,6},{5,7},{14,8},{15,9},{8,1... | collective-permute-start | bytes 393224 | tf_op jit(solution)/shard_map/ppermute | solution.py:21
  6.8 10.5 %collective-permute-start.3 = (bf16[128,512]{1,0:T(8,128)(2,1)S(1)}, bf16[128,512]{1,0:T(8,128)(2,1)S(1)}, u32[]{:S(2)}, u32[]{:S(2)}) collective-permute-start(bf16[128,512]{1,0:T(8,128)(2,1)S(1)} %get-tuple-element.35), channel_id=1, source_target_pairs={{2,0},{3,1},{4,2},{5,3},{6,4},{7,5},{0,6},{1,7},{10,8},{11,9},{12,... | collective-permute-start | bytes 393224 | tf_op jit(solution)/shard_map/ppermute | solution.py:21
  9.8 1.1 %copy-start.5 = (s32[1536,128]{1,0:T(8,128)S(1)}, s32[1536,128]{1,0:T(8,128)}, u32[]{:S(2)}) copy-start(s32[1536,128]{1,0:T(8,128)} %senders.1) | copy-start | bytes 2359300
  10.9 1.1 %copy-start.6 = (s32[1536,128]{1,0:T(8,128)S(1)}, s32[1536,128]{1,0:T(8,128)}, u32[]{:S(2)}) copy-start(s32[1536,128]{1,0:T(8,128)} %receivers.1) | copy-start | bytes 2359300
  12.0 1.7 %copy-start.10 = (bf16[1,1536,512]{2,1,0:T(8,128)(2,1)S(1)}, bf16[1,1536,512]{2,1,0:T(8,128)(2,1)}, u32[]{:S(2)}) copy-start(bf16[1,1536,512]{2,1,0:T(8,128)(2,1)} %param.15) | copy-start | bytes 4718596
  12.3 4.9 %copy-start.14 = (bf16[3072,128]{1,0:T(8,128)(2,1)}, bf16[3072,128]{1,0:T(8,128)(2,1)S(1)}, u32[]{:S(2)}) copy-start(bf16[3072,128]{1,0:T(8,128)(2,1)S(1)} %get-tuple-element.40.flipped) | copy-start | bytes 2359300
  13.7 1.4 %copy-start.12 = (bf16[1,1536,512]{2,1,0:T(8,128)(2,1)S(1)}, bf16[1,1536,512]{2,1,0:T(8,128)(2,1)}, u32[]{:S(2)}) copy-start(bf16[1,1536,512]{2,1,0:T(8,128)(2,1)} %param.18) | copy-start | bytes 4718596
  15.1 2.1 %copy-start.16 = (bf16[1,512,512]{2,1,0:T(8,128)(2,1)S(1)}, bf16[1,512,512]{2,1,0:T(8,128)(2,1)}, u32[]{:S(2)}) copy-start(bf16[1,512,512]{2,1,0:T(8,128)(2,1)} %param.19) | copy-start | bytes 1572868
  15.1 2.1 %copy-start.18 = (f32[1,512]{1,0:T(1,128)S(1)}, f32[1,512]{1,0:T(1,128)}, u32[]{:S(2)}) copy-start(f32[1,512]{1,0:T(1,128)} %gain.6) | copy-start | bytes 6148
  17.3 14.5 %copy-start = (bf16[1,1024,512]{2,1,0:T(8,128)(2,1)S(1)}, bf16[1,1024,512]{2,1,0:T(8,128)(2,1)}, u32[]{:S(2)}) copy-start(bf16[1,1024,512]{2,1,0:T(8,128)(2,1)} %param.21) | copy-start | bytes 3145732
  23.3 44.1 %collective-permute-start.13 = (bf16[1536,512]{1,0:T(8,128)(2,1)}, bf16[1536,512]{1,0:T(8,128)(2,1)}, u32[]{:S(2)}, u32[]{:S(2)}) collective-permute-start(bf16[1536,512]{1,0:T(8,128)(2,1)} %get-tuple-element.50), channel_id=1, source_target_pairs={{0,8},{8,16},{16,24},{1,9},{9,17},{17,25},{2,10},{10,18},{18,26},{... | collective-permute-start | bytes 4718600 | tf_op jit(solution)/shard_map/ppermute | solution.py:26
  25.2 7.3 %collective-permute-start.4 = (bf16[128,512]{1,0:T(8,128)(2,1)S(1)}, bf16[128,512]{1,0:T(8,128)(2,1)S(1)}, u32[]{:S(2)}, u32[]{:S(2)}) collective-permute-start(bf16[128,512]{1,0:T(8,128)(2,1)S(1)} %get-tuple-element.41), channel_id=1, source_target_pairs={{1,0},{2,1},{3,2},{4,3},{5,4},{6,5},{7,6},{0,7},{9,8},{10,9},{11,1... | collective-permute-start | bytes 393224 | tf_op jit(solution)/shard_map/ppermute | solution.py:21
  28.5 5.0 %collective-permute-start.5 = (bf16[128,512]{1,0:T(8,128)(2,1)S(1)}, bf16[128,512]{1,0:T(8,128)(2,1)S(1)}, u32[]{:S(2)}, u32[]{:S(2)}) collective-permute-start(bf16[128,512]{1,0:T(8,128)(2,1)S(1)} %get-tuple-element.42), channel_id=1, source_target_pairs={{7,0},{0,1},{1,2},{2,3},{3,4},{4,5},{5,6},{6,7},{15,8},{8,9},{9,10... | collective-permute-start | bytes 393224 | tf_op jit(solution)/shard_map/ppermute | solution.py:21
  28.5 6.7 %collective-permute-start.6 = (bf16[128,512]{1,0:T(8,128)(2,1)S(1)}, bf16[128,512]{1,0:T(8,128)(2,1)S(1)}, u32[]{:S(2)}, u32[]{:S(2)}) collective-permute-start(bf16[128,512]{1,0:T(8,128)(2,1)S(1)} %get-tuple-element.43), channel_id=1, source_target_pairs={{2,0},{3,1},{4,2},{5,3},{6,4},{7,5},{0,6},{1,7},{10,8},{11,9},{12,... | collective-permute-start | bytes 393224 | tf_op jit(solution)/shard_map/ppermute | solution.py:21
  31.8 7.3 %collective-permute-start.7 = (bf16[128,512]{1,0:T(8,128)(2,1)S(1)}, bf16[128,512]{1,0:T(8,128)(2,1)S(1)}, u32[]{:S(2)}, u32[]{:S(2)}) collective-permute-start(bf16[128,512]{1,0:T(8,128)(2,1)S(1)} %get-tuple-element.44), channel_id=1, source_target_pairs={{6,0},{7,1},{0,2},{1,3},{2,4},{3,5},{4,6},{5,7},{14,8},{15,9},{8,1... | collective-permute-start | bytes 393224 | tf_op jit(solution)/shard_map/ppermute | solution.py:21
  31.8 7.3 %copy-start.3 = (bf16[1,512,512]{2,1,0:T(8,128)(2,1)S(1)}, bf16[1,512,512]{2,1,0:T(8,128)(2,1)}, u32[]{:S(2)}) copy-start(bf16[1,512,512]{2,1,0:T(8,128)(2,1)} %param.22) | copy-start | bytes 1572868
  31.8 7.3 %copy-start.7 = (f32[1,512]{1,0:T(1,128)S(1)}, f32[1,512]{1,0:T(1,128)}, u32[]{:S(2)}) copy-start(f32[1,512]{1,0:T(1,128)} %gain.7) | copy-start | bytes 6148
  31.8 7.2 %copy-start.9 = (s32[1,4]{1,0:T(1,128)S(1)}, s32[1,4]{1,0:T(1,128)}, u32[]{:S(2)}) copy-start(s32[1,4]{1,0:T(1,128)} %param.25) | copy-start | bytes 52
  42.6 17.9 %collective-permute-start.8 = (bf16[1024,512]{1,0:T(8,128)(2,1)}, bf16[1024,512]{1,0:T(8,128)(2,1)S(1)}, u32[]{:S(2)}, u32[]{:S(2)}) collective-permute-start(bf16[1024,512]{1,0:T(8,128)(2,1)} %node.2), channel_id=1, source_target_pairs={{0,8},{8,16},{16,24},{1,9},{9,17},{17,25},{2,10},{10,18},{18,26},{... | collective-permute-start | bytes 3145736 | tf_op jit(solution)/shard_map/ppermute | solution.py:26
  60.5 1.2 %copy-start.4 = (bf16[1024,512]{1,0:T(8,128)(2,1)S(1)}, bf16[1024,512]{1,0:T(8,128)(2,1)}, u32[]{:S(2)}) copy-start(bf16[1024,512]{1,0:T(8,128)(2,1)} %entering.2) | copy-start | bytes 3145732
  61.7 5.7 %copy-start.11 = (bf16[1536,512]{1,0:T(8,128)(2,1)S(1)}, bf16[1536,512]{1,0:T(8,128)(2,1)}, u32[]{:S(2)}) copy-start(bf16[1536,512]{1,0:T(8,128)(2,1)} %entering.3) | copy-start | bytes 4718596
  62.4 10.3 %collective-permute-start.10 = (bf16[128,512]{1,0:T(8,128)(2,1)S(1)}, bf16[128,512]{1,0:T(8,128)(2,1)S(1)}, u32[]{:S(2)}, u32[]{:S(2)}) collective-permute-start(bf16[128,512]{1,0:T(8,128)(2,1)S(1)} %get-tuple-element.47), channel_id=1, source_target_pairs={{1,0},{2,1},{3,2},{4,3},{5,4},{6,5},{7,6},{0,7},{9,8},{10,9},{11,1... | collective-permute-start | bytes 393224 | tf_op jit(solution)/shard_map/ppermute | solution.py:21
  62.4 10.2 %collective-permute-start.11 = (bf16[128,512]{1,0:T(8,128)(2,1)S(1)}, bf16[128,512]{1,0:T(8,128)(2,1)S(1)}, u32[]{:S(2)}, u32[]{:S(2)}) collective-permute-start(bf16[128,512]{1,0:T(8,128)(2,1)S(1)} %get-tuple-element.48), channel_id=1, source_target_pairs={{6,0},{7,1},{0,2},{1,3},{2,4},{3,5},{4,6},{5,7},{14,8},{15,9},{8,1... | collective-permute-start | bytes 393224 | tf_op jit(solution)/shard_map/ppermute | solution.py:21
  62.5 10.2 %collective-permute-start.12 = (bf16[128,512]{1,0:T(8,128)(2,1)S(1)}, bf16[128,512]{1,0:T(8,128)(2,1)S(1)}, u32[]{:S(2)}, u32[]{:S(2)}) collective-permute-start(bf16[128,512]{1,0:T(8,128)(2,1)S(1)} %get-tuple-element.49), channel_id=1, source_target_pairs={{2,0},{3,1},{4,2},{5,3},{6,4},{7,5},{0,6},{1,7},{10,8},{11,9},{12,... | collective-permute-start | bytes 393224 | tf_op jit(solution)/shard_map/ppermute | solution.py:21
  66.3 6.6 %collective-permute-start.9 = (bf16[128,512]{1,0:T(8,128)(2,1)S(1)}, bf16[128,512]{1,0:T(8,128)(2,1)S(1)}, u32[]{:S(2)}, u32[]{:S(2)}) collective-permute-start(bf16[128,512]{1,0:T(8,128)(2,1)S(1)} %get-tuple-element.46), channel_id=1, source_target_pairs={{7,0},{0,1},{1,2},{2,3},{3,4},{4,5},{5,6},{6,7},{15,8},{8,9},{9,10... | collective-permute-start | bytes 393224 | tf_op jit(solution)/shard_map/ppermute | solution.py:21
  67.4 1.4 %copy-start.13 = (bf16[1,1536,512]{2,1,0:T(8,128)(2,1)S(1)}, bf16[1,1536,512]{2,1,0:T(8,128)(2,1)}, u32[]{:S(2)}) copy-start(bf16[1,1536,512]{2,1,0:T(8,128)(2,1)} %param.18) | copy-start | bytes 4718596
  68.8 4.2 %copy-start.15 = (bf16[3072,128]{1,0:T(8,128)(2,1)S(1)}, bf16[3072,128]{1,0:T(8,128)(2,1)}, u32[]{:S(2)}) copy-start(bf16[3072,128]{1,0:T(8,128)(2,1)} %copy-done.14) | copy-start | bytes 2359300
  68.8 4.2 %copy-start.17 = (bf16[1,512,512]{2,1,0:T(8,128)(2,1)S(1)}, bf16[1,512,512]{2,1,0:T(8,128)(2,1)}, u32[]{:S(2)}) copy-start(bf16[1,512,512]{2,1,0:T(8,128)(2,1)} %param.19) | copy-start | bytes 1572868
  68.8 4.2 %copy-start.19 = (f32[1,512]{1,0:T(1,128)S(1)}, f32[1,512]{1,0:T(1,128)}, u32[]{:S(2)}) copy-start(f32[1,512]{1,0:T(1,128)} %gain.6) | copy-start | bytes 6148
  79.0 8.6 %collective-permute-start.14 = (bf16[128,512]{1,0:T(8,128)(2,1)S(1)}, bf16[128,512]{1,0:T(8,128)(2,1)S(1)}, u32[]{:S(2)}, u32[]{:S(2)}) collective-permute-start(bf16[128,512]{1,0:T(8,128)(2,1)S(1)} %get-tuple-element.56), channel_id=1, source_target_pairs={{1,0},{2,1},{3,2},{4,3},{5,4},{6,5},{7,6},{0,7},{9,8},{10,9},{11,1... | collective-permute-start | bytes 393224 | tf_op jit(solution)/shard_map/ppermute | solution.py:21
  81.3 6.3 %collective-permute-start.15 = (bf16[128,512]{1,0:T(8,128)(2,1)S(1)}, bf16[128,512]{1,0:T(8,128)(2,1)S(1)}, u32[]{:S(2)}, u32[]{:S(2)}) collective-permute-start(bf16[128,512]{1,0:T(8,128)(2,1)S(1)} %get-tuple-element.57), channel_id=1, source_target_pairs={{7,0},{0,1},{1,2},{2,3},{3,4},{4,5},{5,6},{6,7},{15,8},{8,9},{9,10... | collective-permute-start | bytes 393224 | tf_op jit(solution)/shard_map/ppermute | solution.py:21
  82.0 7.5 %collective-permute-start.16 = (bf16[128,512]{1,0:T(8,128)(2,1)S(1)}, bf16[128,512]{1,0:T(8,128)(2,1)S(1)}, u32[]{:S(2)}, u32[]{:S(2)}) collective-permute-start(bf16[128,512]{1,0:T(8,128)(2,1)S(1)} %get-tuple-element.58), channel_id=1, source_target_pairs={{2,0},{3,1},{4,2},{5,3},{6,4},{7,5},{0,6},{1,7},{10,8},{11,9},{12,... | collective-permute-start | bytes 393224 | tf_op jit(solution)/shard_map/ppermute | solution.py:21
  86.9 6.8 %collective-permute-start.17 = (bf16[128,512]{1,0:T(8,128)(2,1)S(1)}, bf16[128,512]{1,0:T(8,128)(2,1)S(1)}, u32[]{:S(2)}, u32[]{:S(2)}) collective-permute-start(bf16[128,512]{1,0:T(8,128)(2,1)S(1)} %get-tuple-element.59), channel_id=1, source_target_pairs={{6,0},{7,1},{0,2},{1,3},{2,4},{3,5},{4,6},{5,7},{14,8},{15,9},{8,1... | collective-permute-start | bytes 393224 | tf_op jit(solution)/shard_map/ppermute | solution.py:21
